TPU v7x, 256 devices: a whole 4x4x8 slice. The times are simulated.
256 devices in a mesh: phase: 4 (over x), ctx: 64 (over z, y, core).
Axes of the slice: x: 4, y: 4, z: 8, core: 2. Of those that a mesh axis runs over, the one named last changes fastest.
Arguments:
- hidden: bfloat16 [4, 8192, 4096], P('phase', 'ctx'), may hold values from -6 to 6
- queries: bfloat16 [4, 8192, 2048], P('phase', 'ctx'), may hold values from -400 to 400
- key_value_weight: bfloat16 [4, 4096, 1024], P('phase'), may hold values from -0.09375 to 0.09375
- doc_ids: int32 [4, 8192], P('phase'), may hold values from 0 to 7, never falling along the last dimension, each value on 1 to 6144 neighbouring positions
- scored: int32 [4, 8192], P('phase', 'ctx'), may hold values 0 or 1
Outputs:
- passed: bfloat16 [4, 8192, 2048], P('phase', 'ctx')
Inputs may be any that keep to these rules, and one draw needn't show every extreme that they name: doc_ids never fall along a sequence; one document spans exactly 6144 tokens.
All inputs are finite; a program needn't handle non-finite values. No bound on the sum of `scored` on one device may be relied on, other than what follows from the above.
Results may differ from a plain program's by a relative error of at most 0.008.
The roundings to bfloat16 on the way count: a program that leaves them out, or rounds other values in their place, can miss the bound.
Values may be sent and summed in bfloat16 or wider, within the bound.
A program may use at most 128 MiB of HBM per device.

v0:
```python
import math

import jax
import jax.numpy as jnp
from jax import lax
from jax.sharding import PartitionSpec as P

QUERY_HEADS = 16
KEY_VALUE_HEADS = 4
HEAD_SIZE = 128


rope_base = 500000.0


def from_behind(block, axis, distance):
    devices = range(lax.axis_size(axis))
    route = [((i - distance) % len(devices), i) for i in devices]
    return lax.ppermute(block, axis, route)


def apply_rotary(key_heads, token_positions):
    half_dim = key_heads.shape[-1] // 2
    frequency = rope_base ** (-jnp.arange(half_dim, dtype=jnp.float32) * 2.0 / key_heads.shape[-1])
    angles = token_positions.astype(jnp.float32)[:, None] * frequency[None, :]
    cosine_part = jnp.cos(angles)[:, None, :]
    sine_part = jnp.sin(angles)[:, None, :]
    lower_half = key_heads[..., :half_dim]
    upper_half = key_heads[..., half_dim:]
    return jnp.concatenate(
        [
            lower_half * cosine_part - upper_half * sine_part,
            upper_half * cosine_part + lower_half * sine_part,
        ],
        axis=-1,
    )


def per_device(hidden, queries, key_value_weight, doc_ids, scored):
    count_of_rows = hidden.shape[1]
    first_row = lax.axis_index("ctx") * count_of_rows
    token_positions = first_row + jnp.arange(count_of_rows, dtype=jnp.int32)
    wide = hidden[0].astype(jnp.float32)
    normed = (wide * lax.rsqrt(jnp.mean(wide * wide, axis=-1, keepdims=True) + 1e-05)).astype(
        jnp.bfloat16
    )
    projected_rows = jnp.dot(normed, key_value_weight[0], preferred_element_type=jnp.float32)
    key_value_width = KEY_VALUE_HEADS * HEAD_SIZE
    key_matrix = (
        apply_rotary(
            projected_rows[:, :key_value_width].reshape(count_of_rows, KEY_VALUE_HEADS, HEAD_SIZE),
            token_positions,
        )
        .astype(jnp.bfloat16)
        .reshape(count_of_rows, key_value_width)
    )
    value_matrix = projected_rows[:, key_value_width:].astype(jnp.bfloat16)
    query_group_width = QUERY_HEADS // KEY_VALUE_HEADS
    query_head_count = queries[0].reshape(
        count_of_rows, KEY_VALUE_HEADS, query_group_width, HEAD_SIZE
    )
    sequence_docs = doc_ids[0]
    own_docs = lax.dynamic_slice_in_dim(sequence_docs, first_row, count_of_rows, 0)
    score_scale = 1.0 / math.sqrt(HEAD_SIZE)
    stacked = jnp.concatenate([key_matrix, value_matrix], axis=1)
    collected_rows = lax.all_gather(stacked, "ctx", axis=0, tiled=True)
    sequence_length = collected_rows.shape[0]
    every_key_row = collected_rows[:, :key_value_width].reshape(
        sequence_length, KEY_VALUE_HEADS, HEAD_SIZE
    )
    every_value_row = collected_rows[:, key_value_width:].reshape(
        sequence_length, KEY_VALUE_HEADS, HEAD_SIZE
    )
    head_outputs = []
    for key_value_head in range(KEY_VALUE_HEADS):
        key_part = every_key_row[:, key_value_head : key_value_head + 1]
        key_count = key_part.shape[0]
        scores = (
            jnp.einsum(
                "qhgd,khd->hgqk",
                query_head_count[:, key_value_head : key_value_head + 1],
                key_part,
                preferred_element_type=jnp.float32,
            )
            * score_scale
        )
        key_pos = jnp.arange(key_count, dtype=jnp.int32)
        allowed = (key_pos[None, :] <= token_positions[:, None]) & (
            sequence_docs[None, :] == own_docs[:, None]
        )
        scores = jnp.where(allowed[None, None], scores, jnp.float32(-1e30))
        row_max = jnp.max(scores, axis=-1, keepdims=True)
        expo = jnp.exp(scores - row_max)
        total = jnp.sum(expo, axis=-1)
        weights = expo.astype(jnp.bfloat16)
        summed = jnp.einsum(
            "hgqk,khd->hgqd",
            weights,
            every_value_row[:, key_value_head : key_value_head + 1],
            preferred_element_type=jnp.float32,
        )
        head_outputs.append(summed / total[..., None])
    attended = jnp.transpose(jnp.concatenate(head_outputs, axis=0), (2, 0, 1, 3))
    flat = (
        attended.reshape(count_of_rows, QUERY_HEADS * HEAD_SIZE)
        * scored[0].astype(jnp.float32)[:, None]
    )
    outgoing = flat.astype(jnp.bfloat16)[None]
    return from_behind(outgoing, "phase", 1)


def solution(mesh):
    placed = (
        P("phase", "ctx", None),
        P("phase", "ctx", None),
        P("phase", None, None),
        P("phase", None),
        P("phase", "ctx"),
    )
    return jax.shard_map(
        per_device, mesh=mesh, in_specs=placed, out_specs=P("phase", "ctx", None), check_vma=False
    )
```

profile of v0, /device:TPU:1, one launch (start us, length us, event | category | flops | bytes accessed | tf_op | source)
XLA Modules:
  0.0 297.0 jit_solution(15836771491093661803)
XLA Ops:
  6.5 1.5 fusion.27
  8.1 5.1 %fusion.20 = f32[128,1024]{1,0:T(8,128)S(1)} fusion(bf16[1,4096,1024]{2,1,0:T(8,128)(2,1)} %param.7, bf16[1,128,4096]{2,1,0:T(8,128)(2,1)} %param.5, f32[128]{0:T(128)S(1)} %add_rsqrt_fusion), kind=kOutput, calls=%fused_computation.24 | convolution fusion | flops 1075314688 | bytes 9961984 | tf_op jit(solution)/shard_map/dot_general | solution.py:47
  13.2 0.1 reshape.293
  13.3 0.3 multiply_cosine_fusion
  13.7 0.3 subtract_convert_fusion
  13.9 0.2 pad_maximum_fusion.2
  14.2 0.7 pad_maximum_fusion.1
  14.9 0.3 copy.20
  15.3 3.9 %fusion.26 = pred[128,8192]{0,1:T(8,128)(4,1)S(1)} fusion(s32[128]{0:T(128)S(1)} %dynamic-slice_bitcast_fusion, s32[128]{0:T(128)S(1)} %get-tuple-element.23, s32[8192]{0:T(1024)S(1)} %bitcast.163), kind=kLoop, calls=%fused_computation.31 | loop fusion | flops 3145728 | bytes 1082368 | tf_op jit(solution)/shard_map/and | solution.py:88
  19.2 100.0 %all-gather.2.cloned.1.call-done = bf16[8192,1024]{1,0:T(8,128)(2,1)} async-done(((bf16[128,1024]{1,0:T(8,128)(2,1)}), bf16[8192,1024]{1,0:T(8,128)(2,1)}) %all-gather.2.cloned.1.call-update) | async-done | bytes 16777232 | tf_op jit(solution)/shard_map/all_gather | solution.py:66
  119.2 11.3 %fusion.57 = (bf16[8192,512]{1,0:T(8,128)(2,1)}, bf16[8192,512]{1,0:T(8,128)(2,1)}) fusion(bf16[8192,1024]{1,0:T(8,128)(2,1)} %all-gather.2.cloned.1.call-done), kind=kLoop, calls=%fused_computation.74 | loop fusion | bytes 33554432 | tf_op jit(solution)/shard_map/slice | solution.py:71
  130.5 11.3 %copy.41 = bf16[8192,512]{0,1:T(8,128)(2,1)} copy(bf16[8192,512]{1,0:T(8,128)(2,1)} %get-tuple-element.5) | data formatting | bytes 16777216 | tf_op jit(solution)/shard_map/reshape | solution.py:71
  141.9 12.5 %reshape.294 = bf16[8192,4,128]{2,1,0:T(4,128)(2,1)} reshape(bf16[8192,512]{1,0:T(8,128)(2,1)} %get-tuple-element.6) | data formatting | bytes 16777216 | tf_op jit(solution)/shard_map/reshape | solution.py:68
  154.4 26.4 %fusion.58 = (bf16[8192,1,128]{2,1,0:T(2,128)(2,1)S(1)}, bf16[8192,1,128]{2,1,0:T(2,128)(2,1)S(1)}, bf16[8192,1,128]{2,1,0:T(2,128)(2,1)}, bf16[8192,1,128]{2,1,0:T(2,128)(2,1)S(1)}) fusion(bf16[8192,4,128]{2,1,0:T(4,128)(2,1)} %reshape.294), kind=kLoop, calls=%fused_computation.75 | loop fusion | bytes 16777216 | tf_op jit(solution)/shard_map/slice | solution.py:76
  180.8 7.3 %fusion.62 = (f32[4,128]{1,0:T(4,128)S(1)}, f32[1,4,128,8192]{2,3,1,0:T(8,128)}) fusion(bf16[128,4,4,128]{0,3,2,1:T(8,128)(2,1)S(1)} %bitcast.158, bf16[8192,1,128]{2,1,0:T(2,128)(2,1)S(1)} %get-tuple-element.7, pred[128,8192]{0,1:T(8,128)(4,1)S(1)} %fusion.26), kind=kOutput, calls=%fused_computation.79 | convolution fusion | flops 1086324224 | bytes 22153216 | tf_op jit(solution)/shard_map/qhgd,khd->hgqk/dot_general | solution.py:79
  188.1 7.3 %fusion.60 = (f32[4,128]{1,0:T(4,128)S(1)}, f32[1,4,128,8192]{2,3,1,0:T(8,128)}) fusion(bf16[128,4,4,128]{0,3,2,1:T(8,128)(2,1)S(1)} %bitcast.159, bf16[8192,1,128]{2,1,0:T(2,128)(2,1)S(1)} %get-tuple-element.8, pred[128,8192]{0,1:T(8,128)(4,1)S(1)} %fusion.26), kind=kOutput, calls=%fused_computation.77 | convolution fusion | flops 1086324224 | bytes 22153216 | tf_op jit(solution)/shard_map/qhgd,khd->hgqk/dot_general | solution.py:79
  195.4 8.0 %fusion = f32[4,128]{1,0:T(4,128)S(1)} fusion(f32[1,4,128,8192]{2,3,1,0:T(8,128)} %get-tuple-element.22, f32[4,128]{1,0:T(4,128)S(1)} %get-tuple-element.21), kind=kLoop, calls=%fused_computation.8 | loop fusion | flops 8388096 | bytes 16781312 | tf_op jit(solution)/shard_map/reduce_sum | solution.py:94
  203.4 8.2 %fusion.32 = f32[1,4,128,128]{2,3,1,0:T(8,128)S(1)} fusion(f32[1,4,128,8192]{2,3,1,0:T(8,128)} %get-tuple-element.22, f32[4,128]{1,0:T(4,128)S(1)} %get-tuple-element.21, bf16[8192,4,128]{0,2,1:T(8,128)(2,1)} %bitcast.152, f32[4,128]{1,0:T(4,128)S(1)} %fusion), kind=kOutput, calls=%fused_computation.45 | convolution fusion | flops 1082195968 | bytes 19140608 | tf_op jit(solution)/shard_map/hgqk,khd->hgqd/dot_general | solution.py:96
  211.6 8.0 %fusion.4 = f32[4,128]{1,0:T(4,128)S(1)} fusion(f32[1,4,128,8192]{2,3,1,0:T(8,128)} %get-tuple-element.18, f32[4,128]{1,0:T(4,128)S(1)} %get-tuple-element.17), kind=kLoop, calls=%fused_computation.12 | loop fusion | flops 8388096 | bytes 16781312 | tf_op jit(solution)/shard_map/reduce_sum | solution.py:94
  219.5 8.1 %fusion.44 = f32[1,4,128,128]{2,3,1,0:T(8,128)S(1)} fusion(f32[1,4,128,8192]{2,3,1,0:T(8,128)} %get-tuple-element.18, f32[4,128]{1,0:T(4,128)S(1)} %get-tuple-element.17, bf16[8192,4,128]{0,2,1:T(8,128)(2,1)} %bitcast.153, f32[4,128]{1,0:T(4,128)S(1)} %fusion.4), kind=kOutput, calls=%fused_computation.49 | convolution fusion | flops 1082195968 | bytes 19140608 | tf_op jit(solution)/shard_map/hgqk,khd->hgqd/dot_general | solution.py:96
  227.7 7.3 %fusion.61 = (f32[4,128]{1,0:T(4,128)S(1)}, f32[1,4,128,8192]{2,3,1,0:T(8,128)}) fusion(bf16[128,4,4,128]{0,3,2,1:T(8,128)(2,1)S(1)} %bitcast.160, bf16[8192,1,128]{2,1,0:T(2,128)(2,1)S(1)} %copy-done, pred[128,8192]{0,1:T(8,128)(4,1)S(1)} %fusion.26), kind=kOutput, calls=%fused_computation.78 | convolution fusion | flops 1086324224 | bytes 22153216 | tf_op jit(solution)/shard_map/qhgd,khd->hgqk/dot_general | solution.py:79
  235.0 8.0 %fusion.2 = f32[4,128]{1,0:T(4,128)S(1)} fusion(f32[1,4,128,8192]{2,3,1,0:T(8,128)} %get-tuple-element.20, f32[4,128]{1,0:T(4,128)S(1)} %get-tuple-element.19), kind=kLoop, calls=%fused_computation.10 | loop fusion | flops 8388096 | bytes 16781312 | tf_op jit(solution)/shard_map/reduce_sum | solution.py:94
  243.0 8.0 %fusion.38 = f32[1,4,128,128]{2,3,1,0:T(8,128)S(1)} fusion(f32[1,4,128,8192]{2,3,1,0:T(8,128)} %get-tuple-element.20, f32[4,128]{1,0:T(4,128)S(1)} %get-tuple-element.19, bf16[8192,4,128]{0,2,1:T(8,128)(2,1)} %bitcast.154, f32[4,128]{1,0:T(4,128)S(1)} %fusion.2), kind=kOutput, calls=%fused_computation.47 | convolution fusion | flops 1082195968 | bytes 19140608 | tf_op jit(solution)/shard_map/hgqk,khd->hgqd/dot_general | solution.py:96
  250.9 7.3 %fusion.59 = (f32[4,128]{1,0:T(4,128)S(1)}, f32[1,4,128,8192]{2,3,1,0:T(8,128)}) fusion(bf16[128,4,4,128]{0,3,2,1:T(8,128)(2,1)S(1)} %bitcast.161, bf16[8192,1,128]{2,1,0:T(2,128)(2,1)S(1)} %get-tuple-element.10, pred[128,8192]{0,1:T(8,128)(4,1)S(1)} %fusion.26), kind=kOutput, calls=%fused_computation.76 | convolution fusion | flops 1086324224 | bytes 22153216 | tf_op jit(solution)/shard_map/qhgd,khd->hgqk/dot_general | solution.py:79
  258.3 8.0 %fusion.6 = f32[4,128]{1,0:T(4,128)S(1)} fusion(f32[1,4,128,8192]{2,3,1,0:T(8,128)} %get-tuple-element.16, f32[4,128]{1,0:T(4,128)S(1)} %get-tuple-element.15), kind=kLoop, calls=%fused_computation.14 | loop fusion | flops 8388096 | bytes 16781312 | tf_op jit(solution)/shard_map/reduce_sum | solution.py:94
  266.2 8.0 %fusion.50 = f32[1,4,128,128]{2,3,1,0:T(8,128)S(1)} fusion(f32[1,4,128,8192]{2,3,1,0:T(8,128)} %get-tuple-element.16, f32[4,128]{1,0:T(4,128)S(1)} %get-tuple-element.15, bf16[8192,4,128]{0,2,1:T(8,128)(2,1)} %bitcast.155, f32[4,128]{1,0:T(4,128)S(1)} %fusion.6), kind=kOutput, calls=%fused_computation.51 | convolution fusion | flops 1082195968 | bytes 19140608 | tf_op jit(solution)/shard_map/hgqk,khd->hgqd/dot_general | solution.py:96
  274.2 0.1 pad_maximum_fusion
  274.3 0.3 copy.36
  274.6 0.1 multiply_convert_fusion
  274.8 1.3 collective-permute-start
  276.0 13.3 %collective-permute-done = bf16[1,128,2048]{2,1,0:T(8,128)(2,1)S(1)} collective-permute-done((bf16[1,128,2048]{2,1,0:T(8,128)(2,1)S(1)}, bf16[1,128,2048]{2,1,0:T(8,128)(2,1)S(1)}, u32[]{:S(2)}, u32[]{:S(2)}) %collective-permute-start) | collective-permute-done | bytes 524320 | tf_op jit(solution)/shard_map/ppermute | solution.py:19
  289.3 0.8 copy.70
  (18 shorter events, 0.1 us)
Async XLA Ops:
  6.5 112.7 %all-gather.2.cloned.1.call-start = ((), (), s32[]{:S(2)}) async-start(), calls=%async_computation | async-start | bytes 17039360 | tf_op jit(solution)/shard_map/all_gather | solution.py:66
  8.1 6.8 %copy-start.1 = (bf16[1,128,2048]{2,1,0:T(8,128)(2,1)S(1)}, bf16[1,128,2048]{2,1,0:T(8,128)(2,1)}, u32[]{:S(2)}) copy-start(bf16[1,128,2048]{2,1,0:T(8,128)(2,1)} %param.6) | copy-start | bytes 1572868
  8.1 7.1 %copy-start.2 = (s32[1,8192]{1,0:T(1,128)S(1)}, s32[1,8192]{1,0:T(1,128)}, u32[]{:S(2)}) copy-start(s32[1,8192]{1,0:T(1,128)} %param.8) | copy-start | bytes 98308
  8.1 7.1 %copy-start.3 = (s32[1,128]{1,0:T(1,128)S(1)}, s32[1,128]{1,0:T(1,128)}, u32[]{:S(2)}) copy-start(s32[1,128]{1,0:T(1,128)} %param.9) | copy-start | bytes 1540
  219.5 8.1 %copy-start = (bf16[8192,1,128]{2,1,0:T(2,128)(2,1)S(1)}, bf16[8192,1,128]{2,1,0:T(2,128)(2,1)}, u32[]{:S(2)}) copy-start(bf16[8192,1,128]{2,1,0:T(2,128)(2,1)} %get-tuple-element.9) | copy-start | bytes 6291460
  274.8 14.6 %collective-permute-start = (bf16[1,128,2048]{2,1,0:T(8,128)(2,1)S(1)}, bf16[1,128,2048]{2,1,0:T(8,128)(2,1)S(1)}, u32[]{:S(2)}, u32[]{:S(2)}) collective-permute-start(bf16[1,128,2048]{2,1,0:T(8,128)(2,1)S(1)} %multiply_convert_fusion), channel_id=1, source_target_pairs={{192,0},{0,64},{64,128},{128,192},{193,1},{1,65},{65,129},{129,193... | collective-permute-start | bytes 1572872 | tf_op jit(solution)/shard_map/ppermute | solution.py:19
Sparse Core Ops, SparseCore 0:
  15.0 104.1 all-gather.1
where the time goes:
time: 298 us; the launch traced here: 297 us
  waiting for transfers between devices  113 us (38%)
  matrix products  66.5 us (22%)
  local copies, waits for them, and re-layouts  63.2 us (21%)
  other arithmetic  39.1 us (13%)
  between operations  13.6 us (5%)
    all_gather x1, waiting for transfers between devices, per_device(): collected_rows = lax.all_gather(stacked, 'ctx', axis=0, tiled=True)  100 us
    dot_general x4, matrix products, per_device(): jnp.einsum('hgqk,khd->hgqd', weights, every_value_row[:, key_value_head:k...  32.2 us
    reduce_sum x4, other arithmetic, per_device(): total = jnp.sum(expo, axis=-1)  31.9 us
    dot_general x4, matrix products, per_device(): jnp.einsum('qhgd,khd->hgqk', query_head_count[:, key_value_head:key_value...  29.2 us
    slice x1, local copies, waits for them, and re-layouts, per_device(): key_part = every_key_row[:, key_value_head:key_value_head + 1]  26.4 us
    ppermute x1, waiting for transfers between devices, from_behind(): return lax.ppermute(block, axis, route)  13.3 us
    reshape x1, local copies, waits for them, and re-layouts, per_device(): collected_rows[:, :key_value_width]  12.5 us
    slice x1, local copies, waits for them, and re-layouts, per_device(): collected_rows[:, key_value_width:]  11.3 us
  transfers between devices with their start and end apart: 2, of which 2 were waited for; matrix products, arithmetic and copies ran while one was open for 1% of the time, Pallas kernels for 0%

commit v1 on v0

v1 whole, which is shorter than its diff:
```python
import functools
import math

import jax
import jax.numpy as jnp
from jax import lax
from jax.experimental import pallas as pl
from jax.experimental.pallas import tpu as pltpu
from jax.sharding import PartitionSpec as P

KEY_VALUE_HEADS = 4
GROUP = 4
HEAD_SIZE = 128
ROPE_BASE = 500000.0
PHASES = 4
NZ, NY, NC = 8, 4, 2
ROWS = 128
MODEL_WIDTH = 4096
DEPTH_STEP = 1024
MESH = pl.DeviceIdType.MESH
FAR = -float(2.0**100)
SCALE = 1.0 / math.sqrt(HEAD_SIZE)
ANY = pl.BlockSpec(memory_space=pl.ANY)
VMEM = pl.BlockSpec(memory_space=pltpu.VMEM)


def project(hidden_ref, weight_ref, cos_ref, sin_ref, out_ref, normed, acc):
    step = pl.program_id(0)

    @pl.when(step == 0)
    def _():
        wide = hidden_ref[0].astype(jnp.float32)
        scale = lax.rsqrt(jnp.mean(wide * wide, axis=-1, keepdims=True) + 1e-05)
        rows = (wide * scale).astype(jnp.bfloat16)
        for i in range(MODEL_WIDTH // DEPTH_STEP):
            normed[i] = rows[:, i * DEPTH_STEP : (i + 1) * DEPTH_STEP]
        acc[...] = jnp.zeros_like(acc)

    acc[...] += jnp.dot(normed[step], weight_ref[0], preferred_element_type=jnp.float32)

    @pl.when(step == pl.num_programs(0) - 1)
    def _():
        cos, sin = cos_ref[...], sin_ref[...]
        half = HEAD_SIZE // 2
        for h in range(KEY_VALUE_HEADS):
            keys = acc[:, h * HEAD_SIZE : (h + 1) * HEAD_SIZE]
            low, high = keys[:, :half], keys[:, half:]
            turned = jnp.concatenate([low * cos - high * sin, high * cos + low * sin], axis=-1)
            out_ref[h, 0] = jnp.transpose(turned).astype(jnp.bfloat16)
            at = (KEY_VALUE_HEADS + h) * HEAD_SIZE
            out_ref[h, 1] = acc[:, at : at + HEAD_SIZE].astype(jnp.bfloat16)


def place():
    x = lax.axis_index("phase")
    at = lax.axis_index("ctx")
    z = at // (NY * NC)
    y = lax.rem(at // NC, NY)
    c = lax.rem(at, NC)
    return x, z, y, c


def device(x, z, y, c):
    return (x, (z * NY + y) * NC + c)


def gather(
    kvp, q, docs, scored, kv, q4, docs_out, scored_out,
    a_send, a_recv, q_send, q_recv, s_send, s_recv, up_send, up_recv, dn_send, dn_recv, p_send, p_recv,
):
    x, z, y, c = place()
    xn, xp = lax.rem(x + 1, PHASES), lax.rem(x + PHASES - 1, PHASES)
    zu, zd = lax.rem(z + 1, NZ), lax.rem(z + NZ - 1, NZ)
    barrier = pltpu.get_barrier_semaphore()
    for y2 in range(NY):
        pl.semaphore_signal(barrier, inc=1, device_id=device(xp, z, y2, c), device_id_type=MESH)
    for who in (device(x, zu, y, c), device(x, zd, y, c), device(x, z, y, 1 - c)):
        pl.semaphore_signal(barrier, inc=1, device_id=who, device_id_type=MESH)
    pl.semaphore_wait(barrier, NY + 3)

    def remote(src, dst, send, recv, who):
        return pltpu.make_async_remote_copy(
            src_ref=src, dst_ref=dst, send_sem=send, recv_sem=recv, device_id=who, device_id_type=MESH
        )

    started = []

    def go(copy):
        copy.start()
        started.append(copy)
        return copy

    first = [
        go(remote(kvp.at[h], kv.at[c, z, y], a_send.at[h], a_recv.at[y], device(xn, z, h, c)))
        for h in range(NY)
    ]
    small = [
        go(remote(docs, docs_out, s_send.at[0], s_recv.at[0], device(xn, z, y, c))),
        go(remote(scored, scored_out, s_send.at[1], s_recv.at[1], device(xn, z, y, c))),
    ]
    asked = [
        go(
            remote(
                q.at[0, :, pl.ds(h * GROUP * HEAD_SIZE, GROUP * HEAD_SIZE)],
                q4.at[y], q_send.at[h], q_recv.at[y], device(xn, z, h, c),
            )
        )
        for h in range(NY)
    ]

    def slot(r, p):
        return kv.at[c, lax.rem(z + r + NZ, NZ), p]

    def arrived(ref, sem):
        remote(ref, ref, sem, sem, device(x, z, y, 1 - c)).wait_recv()

    def partner(r, p):
        ref = slot(r, p)
        i = (r + NZ) % NZ
        go(remote(ref, ref, p_send.at[i, p], p_recv.at[i, p], device(x, z, y, 1 - c)))

    def up(k, p):
        ref = slot(-(k - 1), p)
        go(remote(ref, ref, up_send.at[k - 1, p], up_recv.at[k - 1, p], device(x, zu, y, c)))

    def down(k, p):
        ref = slot(k - 1, p)
        go(remote(ref, ref, dn_send.at[k - 1, p], dn_recv.at[k - 1, p], device(x, zd, y, c)))

    ups = {1: (0, 1, 2, 3), 2: (0, 1, 2, 3), 3: (0, 1, 2, 3), 4: (0, 1)}
    downs = {1: (0, 1, 2, 3), 2: (0, 1, 2, 3), 3: (0, 1, 2, 3), 4: (2, 3)}
    for p in range(NY):
        arrived(slot(0, p), a_recv.at[p])
        up(1, p)
        down(1, p)
        partner(0, p)
    for k in range(1, 5):
        for p in range(NY):
            if p in ups[k]:
                arrived(slot(-k, p), up_recv.at[k - 1, p])
                if k < 4 and p in ups[k + 1]:
                    up(k + 1, p)
                partner(-k, p)
            if p in downs[k]:
                arrived(slot(k, p), dn_recv.at[k - 1, p])
                if k < 4 and p in downs[k + 1]:
                    down(k + 1, p)
                partner(k, p)
    for r in range(NZ):
        for p in range(NY):
            arrived(kv.at[1 - c, lax.rem(z + r, NZ), p], p_recv.at[r, p])
    for p in range(NY):
        arrived(q4.at[p], q_recv.at[p])
    arrived(docs_out, s_recv.at[0])
    arrived(scored_out, s_recv.at[1])
    for copy in started:
        copy.wait_send()


CHUNK = NC * NY * ROWS


def attend(kv, q4, docs, out, qaug, kaug, vaug, acc, top):
    x, z, y, c = place()
    plane = NY * NC * ROWS
    lanes = lax.broadcasted_iota(jnp.int32, (ROWS, ROWS), 1)
    sublanes = lax.broadcasted_iota(jnp.int32, (ROWS, ROWS), 0)
    apart = jnp.where(lanes == sublanes, 0.0, FAR).astype(jnp.bfloat16)
    for j in range(NY):
        at = pl.multiple_of(z * plane + (j * NC + c) * ROWS, ROWS)
        mine = docs[:, pl.ds(at, ROWS)]
        hot = (sublanes == mine).astype(jnp.bfloat16)
        away = lax.dot_general(
            hot, apart, (((0,), (0,)), ((), ())), preferred_element_type=jnp.float32
        ).astype(jnp.bfloat16)
        for g in range(GROUP):
            r = (j * GROUP + g) * ROWS
            qaug[r : r + ROWS, :HEAD_SIZE] = q4[j, :, g * HEAD_SIZE : (g + 1) * HEAD_SIZE]
            qaug[r : r + ROWS, HEAD_SIZE:] = away
    vaug[:, HEAD_SIZE:] = jnp.ones((CHUNK, HEAD_SIZE), jnp.bfloat16)

    def load(zk):
        for c2 in range(NC):
            for p in range(NY):
                i = (c2 * NY + p) * ROWS
                kaug[:HEAD_SIZE, i : i + ROWS] = kv[c2, zk, p, 0]
                at = pl.multiple_of(zk * plane + (p * NC + c2) * ROWS, ROWS)
                kaug[HEAD_SIZE:, i : i + ROWS] = (sublanes == docs[:, pl.ds(at, ROWS)]).astype(jnp.bfloat16)
                vaug[i : i + ROWS, :HEAD_SIZE] = kv[c2, zk, p, 1]

    unit = 2 * ROWS

    def scores_of(rows):
        return jnp.dot(qaug[rows, :], kaug[...], preferred_element_type=jnp.float32)

    load(z)

    @pl.loop(0, NY * GROUP * ROWS // unit)
    def _(u):
        rows = pl.ds(pl.multiple_of(u * unit, unit), unit)
        s = scores_of(rows)
        key = lax.broadcasted_iota(jnp.int32, (1, CHUNK), 1)
        key = (lax.rem(key // ROWS, NY) * NC + key // (NY * ROWS)) * ROWS + lax.rem(key, ROWS)
        row = lax.broadcasted_iota(jnp.int32, (unit, 1), 0)
        own = (u // 2 * NC + c) * ROWS + lax.rem(row, ROWS)
        s = jnp.where(key <= own, s, -1e30)
        m = jnp.max(s, axis=-1, keepdims=True)
        w = jnp.exp((s - m) * SCALE).astype(jnp.bfloat16)
        acc[rows, :] = jnp.dot(w, vaug[...], preferred_element_type=jnp.float32)
        top[rows, :] = jnp.broadcast_to(m, (unit, HEAD_SIZE))

    at = pl.multiple_of(z * plane, ROWS)
    head_doc = docs[:, pl.ds(at, ROWS)][:, :1]
    start = jnp.sum((docs[...] < head_doc).astype(jnp.int32))

    @pl.loop(start // plane, z)
    def _(zk):
        load(zk)

        @pl.loop(0, NY * GROUP * ROWS // unit)
        def _(u):
            rows = pl.ds(pl.multiple_of(u * unit, unit), unit)
            s = scores_of(rows)
            before = top[rows, :1]
            m = jnp.maximum(before, jnp.max(s, axis=-1, keepdims=True))
            w = jnp.exp((s - m) * SCALE).astype(jnp.bfloat16)
            fade = jnp.exp((before - m) * SCALE)
            acc[rows, :] = acc[rows, :] * fade + jnp.dot(w, vaug[...], preferred_element_type=jnp.float32)
            top[rows, :] = jnp.broadcast_to(m, (unit, HEAD_SIZE))

    for j in range(NY):
        for g in range(GROUP):
            r = (j * GROUP + g) * ROWS
            out[j, :, g * HEAD_SIZE : (g + 1) * HEAD_SIZE] = (
                acc[r : r + ROWS, :HEAD_SIZE] / acc[r : r + ROWS, HEAD_SIZE:]
            ).astype(jnp.bfloat16)


def give_back(o, out, send, recv, local):
    x, z, y, c = place()
    barrier = pltpu.get_barrier_semaphore()
    for d in range(1, NY):
        pl.semaphore_signal(
            barrier, inc=1, device_id=device(x, z, lax.rem(y + d, NY), c), device_id_type=MESH
        )
    pl.semaphore_wait(barrier, NY - 1)
    keep = pltpu.make_async_copy(o.at[y], out.at[y], local)
    copies = []
    for d in (2, 1, 3):
        to = lax.rem(y + d, NY)
        copy = pltpu.make_async_remote_copy(
            src_ref=o.at[to], dst_ref=out.at[y], send_sem=send.at[d - 1], recv_sem=recv.at[d - 1],
            device_id=device(x, z, to, c), device_id_type=MESH,
        )
        copy.start()
        copies.append(copy)
    keep.start()
    keep.wait()
    for copy in copies:
        copy.wait()


def per_device(hidden, queries, key_value_weight, doc_ids, scored):
    first_row = lax.axis_index("ctx") * ROWS
    positions = first_row + jnp.arange(ROWS, dtype=jnp.int32)
    half = HEAD_SIZE // 2
    frequency = ROPE_BASE ** (-jnp.arange(half, dtype=jnp.float32) * 2.0 / HEAD_SIZE)
    angles = positions.astype(jnp.float32)[:, None] * frequency[None, :]
    kvp = pl.pallas_call(
        project,
        grid=(MODEL_WIDTH // DEPTH_STEP,),
        in_specs=[
            pl.BlockSpec((1, ROWS, MODEL_WIDTH), lambda i: (0, 0, 0)),
            pl.BlockSpec((1, DEPTH_STEP, 1024), lambda i: (0, i, 0)),
            pl.BlockSpec((ROWS, half), lambda i: (0, 0)),
            pl.BlockSpec((ROWS, half), lambda i: (0, 0)),
        ],
        out_specs=pl.BlockSpec((NY, 2, ROWS, HEAD_SIZE), lambda i: (0, 0, 0, 0)),
        out_shape=jax.ShapeDtypeStruct((NY, 2, ROWS, HEAD_SIZE), jnp.bfloat16),
        scratch_shapes=[
            pltpu.VMEM((MODEL_WIDTH // DEPTH_STEP, ROWS, DEPTH_STEP), jnp.bfloat16),
            pltpu.VMEM((ROWS, 1024), jnp.float32),
        ],
        name="project",
    )(hidden, key_value_weight, jnp.cos(angles), jnp.sin(angles))

    dma = pltpu.SemaphoreType.DMA
    kv, q4, docs, marks = pl.pallas_call(
        gather,
        in_specs=[ANY] * 4,
        out_specs=[ANY] * 4,
        out_shape=[
            jax.ShapeDtypeStruct((NC, NZ, NY, 2, ROWS, HEAD_SIZE), jnp.bfloat16),
            jax.ShapeDtypeStruct((NY, ROWS, GROUP * HEAD_SIZE), jnp.bfloat16),
            jax.ShapeDtypeStruct(doc_ids.shape, jnp.int32),
            jax.ShapeDtypeStruct(scored.shape, jnp.int32),
        ],
        scratch_shapes=[
            dma((NY,)), dma((NY,)), dma((NY,)), dma((NY,)), dma((2,)), dma((2,)),
            dma((4, NY)), dma((4, NY)), dma((4, NY)), dma((4, NY)), dma((NZ, NY)), dma((NZ, NY)),
        ],
        compiler_params=pltpu.CompilerParams(collective_id=0, has_side_effects=True),
        name="gather",
    )(kvp, queries, doc_ids, scored)

    o = pl.pallas_call(
        attend,
        in_specs=[VMEM] * 3,
        out_specs=VMEM,
        out_shape=jax.ShapeDtypeStruct((NY, ROWS, GROUP * HEAD_SIZE), jnp.bfloat16),
        scratch_shapes=[
            pltpu.VMEM((NY * GROUP * ROWS, 2 * HEAD_SIZE), jnp.bfloat16),
            pltpu.VMEM((2 * HEAD_SIZE, CHUNK), jnp.bfloat16),
            pltpu.VMEM((CHUNK, 2 * HEAD_SIZE), jnp.bfloat16),
            pltpu.VMEM((NY * GROUP * ROWS, 2 * HEAD_SIZE), jnp.float32),
            pltpu.VMEM((NY * GROUP * ROWS, HEAD_SIZE), jnp.float32),
        ],
        name="attend",
    )(kv, q4, docs)

    back = pl.pallas_call(
        give_back,
        in_specs=[ANY],
        out_specs=ANY,
        out_shape=jax.ShapeDtypeStruct((NY, ROWS, GROUP * HEAD_SIZE), jnp.bfloat16),
        scratch_shapes=[dma((NY - 1,)), dma((NY - 1,)), dma],
        compiler_params=pltpu.CompilerParams(collective_id=1, has_side_effects=True),
        name="give_back",
    )(o)
    flat = jnp.transpose(back, (1, 0, 2)).reshape(ROWS, NY * GROUP * HEAD_SIZE)
    return (flat * marks[0].astype(jnp.bfloat16)[:, None])[None]


def solution(mesh):
    placed = (
        P("phase", "ctx", None),
        P("phase", "ctx", None),
        P("phase", None, None),
        P("phase", None),
        P("phase", "ctx"),
    )
    return jax.shard_map(
        per_device, mesh=mesh, in_specs=placed, out_specs=P("phase", "ctx", None), check_vma=False
    )
```

time: 298 us -> 118 us (0.40)
  the two profiles are of different devices: /device:TPU:1 before, /device:TPU:196 now
where the time goes in v1:
time: 118 us
  Pallas kernels  114 us (97%)
  local copies, waits for them, and re-layouts  2.32 us (2%)
  other arithmetic  1.7 us (1%)
    pallas_call x1, Pallas kernels, per_device(): pl.pallas_call(attend, in_specs=[VMEM] * 3, out_specs=VMEM, out_shape=jax...  59.2 us
    pallas_call x1, Pallas kernels, per_device(): pl.pallas_call(gather, in_specs=[ANY] * 4, out_specs=[ANY] * 4, out_shape...  33.2 us
    pallas_call x1, Pallas kernels, per_device(): pl.pallas_call(give_back, in_specs=[ANY], out_specs=ANY, out_shape=jax.Sh...  14.6 us
    pallas_call x1, Pallas kernels, per_device(): pl.pallas_call(project, grid=(MODEL_WIDTH // DEPTH_STEP,), in_specs=[pl.B...  6.71 us

profile of v1, /device:TPU:196, one launch (start us, length us, event | category | flops | bytes accessed | tf_op | source)
XLA Modules:
  0.0 117.9 jit_solution(2996354404898568117)
XLA Ops:
  0.0 1.0 multiply_sine_fusion
  1.0 6.7 %project.1.kvp = bf16[4,2,128,128]{3,2,1,0:T(8,128)(2,1)} custom-call(bf16[1,128,4096]{2,1,0:T(8,128)(2,1)} %hidden_ref.1, bf16[1,4096,1024]{2,1,0:T(8,128)(2,1)} %weight_ref.1, f32[128,64]{1,0:T(8,128)} %get-tuple-element.14.cos_ref, f32[128,64]{1,0:T(8,128)} %get-tuple-element.13.sin_ref), custom_call_target="tpu_custom_call" | custom-call | tf_op jit(solution)/shard_map/project/pallas_call | solution.py:269
  7.7 33.2 %gather.1 = (bf16[2,8,4,2,128,128]{5,4,3,2,1,0:T(8,128)(2,1)}, bf16[4,128,512]{2,1,0:T(8,128)(2,1)}, s32[1,8192]{1,0:T(1,128)}, s32[1,128]{1,0:T(1,128)}) custom-call(bf16[4,2,128,128]{3,2,1,0:T(8,128)(2,1)} %project.1.kvp, bf16[1,128,2048]{2,1,0:T(8,128)(2,1)} %q.1, s32[1,8192]{1,0:T(1,128)} %docs.1, s32[1,128]{1,0:T(1,128)} %scored.1), custom_call_target="tpu_custom_call" | custom-call | tf_op jit(solution)/shard_map/gather/pallas_call | solution.py:288
  40.9 59.2 %attend.1.o = bf16[4,128,512]{2,1,0:T(8,128)(2,1)} custom-call(bf16[2,8,4,2,128,128]{5,4,3,2,1,0:T(8,128)(2,1)} %get-tuple-element.9.kv, bf16[4,128,512]{2,1,0:T(8,128)(2,1)} %get-tuple-element.10.q4, s32[1,8192]{1,0:T(1,128)} %get-tuple-element.11.docs), custom_call_target="tpu_custom_call" | custom-call | tf_op jit(solution)/shard_map/attend/pallas_call | solution.py:306
  100.2 14.6 %give_back.1 = bf16[4,128,512]{2,1,0:T(8,128)(2,1)} custom-call(bf16[4,128,512]{2,1,0:T(8,128)(2,1)} %attend.1.o), custom_call_target="tpu_custom_call" | custom-call | tf_op jit(solution)/shard_map/give_back/pallas_call | solution.py:321
  114.8 1.3 %copy.6 = bf16[128,4,512]{0,2,1:T(8,128)(2,1)S(1)} copy(bf16[128,4,512]{2,0,1:T(8,128)(2,1)} %bitcast.5) | data formatting | bytes 1048576 | tf_op jit(solution)/shard_map/transpose | solution.py:330
  116.1 0.7 convert_bitcast_fusion
  116.8 0.1 bitcast_multiply_fusion
  116.9 1.0 copy.7
  (2 shorter events, 0.0 us)

commit v2 on v0

v2 whole, which is shorter than its diff:
```python
import math

import jax
import jax.numpy as jnp
from jax import lax
from jax.experimental import pallas as pl
from jax.experimental.pallas import tpu as pltpu
from jax.sharding import PartitionSpec as P

KEY_VALUE_HEADS = 4
HEAD_SIZE = 128
ROPE_BASE = 500000.0
PHASES = 4
NZ, NY, NC = 8, 4, 2
ROWS = 128
MODEL_WIDTH = 4096
DEPTH_STEP = 512
MESH = pl.DeviceIdType.MESH
FAR = -float(2.0**100)
SCALE = math.log2(math.e) / math.sqrt(HEAD_SIZE)
ORDER = (0, 1, 7, 2, 6, 3, 5, 4)
WIDTH = 2 * HEAD_SIZE
CHUNK = NC * NY * ROWS
ANY = pl.BlockSpec(memory_space=pl.ANY)
VMEM = pl.BlockSpec(memory_space=pltpu.VMEM)


def place():
    x = lax.axis_index("phase")
    at = lax.axis_index("ctx")
    z = at // (NY * NC)
    y = lax.rem(at // NC, NY)
    c = lax.rem(at, NC)
    return x, z, y, c


def device(x, z, y, c):
    return (x, (z * NY + y) * NC + c)


def remote(src, dst, send, recv, who):
    return pltpu.make_async_remote_copy(
        src_ref=src, dst_ref=dst, send_sem=send, recv_sem=recv, device_id=who, device_id_type=MESH
    )


def gather(
    hidden, weight, q, cos_ref, sin_ref, kv, q8,
    wbuf, kvp, acc, own, w_sem, l_sem,
    a_send, a_recv, q_send, q_recv, up_send, up_recv, dn_send, dn_recv, p_send, p_recv,
):
    x, z, y, c = place()
    yu, yd = lax.rem(y + 1, NY), lax.rem(y + NY - 1, NY)
    loads = []
    for i in range(MODEL_WIDTH // DEPTH_STEP):
        part = pl.ds(i * DEPTH_STEP, DEPTH_STEP)
        load = pltpu.make_async_copy(weight.at[0, part], wbuf.at[part], w_sem.at[i])
        load.start()
        loads.append(load)
    barrier = pltpu.get_barrier_semaphore()
    for d in range(1, NZ):
        pl.semaphore_signal(
            barrier, inc=1, device_id=device(x, lax.rem(z + d, NZ), y, c), device_id_type=MESH
        )
    for who in (device(x, z, yu, c), device(x, z, yd, c), device(x, z, y, 1 - c)):
        pl.semaphore_signal(barrier, inc=1, device_id=who, device_id_type=MESH)
    pl.semaphore_wait(barrier, NZ - 1 + 3)

    started = []

    def go(copy):
        copy.start()
        started.append(copy)

    def columns(at):
        return q.at[0, :, pl.ds(pl.multiple_of(at * WIDTH, WIDTH), WIDTH)]

    for d in ORDER[1:]:
        to = lax.rem(z + d, NZ)
        go(remote(columns(to), q8.at[z], q_send.at[d], q_recv.at[z], device(x, to, y, c)))
    keep = pltpu.make_async_copy(columns(z), own, l_sem.at[0])
    keep.start()

    wide = hidden[0].astype(jnp.float32)
    scale = lax.rsqrt(jnp.mean(wide * wide, axis=-1, keepdims=True) + 1e-05)
    rows = (wide * scale).astype(jnp.bfloat16)
    for i, load in enumerate(loads):
        load.wait()
        term = jnp.dot(
            rows[:, i * DEPTH_STEP : (i + 1) * DEPTH_STEP],
            wbuf[i * DEPTH_STEP : (i + 1) * DEPTH_STEP, :],
            preferred_element_type=jnp.float32,
        )
        if i == 0:
            acc[...] = term
        else:
            acc[...] += term
    cos, sin = cos_ref[...], sin_ref[...]
    half = HEAD_SIZE // 2
    for h in range(KEY_VALUE_HEADS):
        keys = acc[:, h * HEAD_SIZE : (h + 1) * HEAD_SIZE]
        low, high = keys[:, :half], keys[:, half:]
        turned = jnp.concatenate([low * cos - high * sin, high * cos + low * sin], axis=-1)
        kvp[h, 0] = jnp.transpose(turned).astype(jnp.bfloat16)
        at = (KEY_VALUE_HEADS + h) * HEAD_SIZE
        kvp[h, 1] = acc[:, at : at + HEAD_SIZE].astype(jnp.bfloat16)

    keep.wait()
    put = pltpu.make_async_copy(own, q8.at[z], l_sem.at[1])
    put.start()

    for d in ORDER[1:]:
        to = lax.rem(z + d, NZ)
        go(remote(kvp.at[to // 2], kv.at[c, y, z], a_send.at[d], a_recv.at[z], device(x, to, y, c)))
    mine = kvp.at[z // 2]
    home = pltpu.make_async_copy(mine, kv.at[c, y, z], l_sem.at[2])
    home.start()

    def slot(r, d):
        return kv.at[c, lax.rem(y + r + NY, NY), lax.rem(z + d, NZ)]

    def arrived(ref, sem):
        remote(ref, ref, sem, sem, device(x, z, y, 1 - c)).wait_recv()

    def partner(r, d, ref=None):
        i = (r + NY) % NY
        src = slot(r, d) if ref is None else ref
        go(remote(src, slot(r, d), p_send.at[i, d], p_recv.at[i, d], device(x, z, y, 1 - c)))

    def up(k, d, ref=None):
        dst = slot(1 - k, d)
        src = dst if ref is None else ref
        go(remote(src, dst, up_send.at[k - 1, d], up_recv.at[k - 1, d], device(x, z, yu, c)))

    def down(k, d, ref=None):
        dst = slot(k - 1, d)
        src = dst if ref is None else ref
        go(remote(src, dst, dn_send.at[k - 1, d], dn_recv.at[k - 1, d], device(x, z, yd, c)))

    far_up, far_down = ORDER[0::2], ORDER[1::2]
    for d in ORDER:
        if d == 0:
            up(1, d, mine)
            down(1, d, mine)
            partner(0, d, mine)
        else:
            arrived(slot(0, d), a_recv.at[lax.rem(z + d, NZ)])
            up(1, d)
            down(1, d)
            partner(0, d)
    for d in ORDER:
        arrived(slot(-1, d), up_recv.at[0, d])
        if d in far_up:
            up(2, d)
        partner(-1, d)
        arrived(slot(1, d), dn_recv.at[0, d])
        if d in far_down:
            down(2, d)
        partner(1, d)
    for d in ORDER:
        if d in far_up:
            arrived(slot(2, d), up_recv.at[1, d])
        else:
            arrived(slot(2, d), dn_recv.at[1, d])
        partner(2, d)
    for r in range(NY):
        for d in ORDER:
            arrived(kv.at[1 - c, lax.rem(y + r, NY), lax.rem(z + d, NZ)], p_recv.at[r, d])
    for d in ORDER[1:]:
        at = lax.rem(z + d, NZ)
        arrived(q8.at[at], q_recv.at[at])
    put.wait()
    home.wait()
    for copy in started:
        copy.wait_send()


UNIT = 2 * ROWS


def attend(kv, q8, docs, out, qaug, kaug, vaug, acc, top):
    x, z, y, c = place()
    lanes = lax.broadcasted_iota(jnp.int32, (ROWS, ROWS), 1)
    sublanes = lax.broadcasted_iota(jnp.int32, (ROWS, ROWS), 0)
    apart = jnp.where(lanes == sublanes, 0.0, FAR).astype(jnp.bfloat16)
    block = y * NC + c

    @pl.loop(0, NZ)
    def _(i):
        at = pl.multiple_of(i * CHUNK + block * ROWS, ROWS)
        hot = (sublanes == docs[:, pl.ds(at, ROWS)]).astype(jnp.bfloat16)
        away = lax.dot_general(
            hot, apart, (((0,), (0,)), ((), ())), preferred_element_type=jnp.float32
        ).astype(jnp.bfloat16)
        for g in range(2):
            qaug[i, g * ROWS : (g + 1) * ROWS, :HEAD_SIZE] = q8[i, :, g * HEAD_SIZE : (g + 1) * HEAD_SIZE]
            qaug[i, g * ROWS : (g + 1) * ROWS, HEAD_SIZE:] = away
        vaug[i, :, HEAD_SIZE:] = jnp.ones((CHUNK, HEAD_SIZE), jnp.bfloat16)
        for p in range(NY):
            for c2 in range(NC):
                b = (p * NC + c2) * ROWS
                at = pl.multiple_of(i * CHUNK + b, ROWS)
                kaug[i, :HEAD_SIZE, b : b + ROWS] = kv[c2, p, i, 0]
                kaug[i, HEAD_SIZE:, b : b + ROWS] = (sublanes == docs[:, pl.ds(at, ROWS)]).astype(jnp.bfloat16)
                vaug[i, b : b + ROWS, :HEAD_SIZE] = kv[c2, p, i, 1]

    def scores(i, k):
        return jnp.dot(qaug[i], kaug[k], preferred_element_type=jnp.float32)

    def first(i):
        s = scores(i, i)
        key = lax.broadcasted_iota(jnp.int32, (1, CHUNK), 1)
        row = lax.broadcasted_iota(jnp.int32, (UNIT, 1), 0)
        s = jnp.where(key <= block * ROWS + lax.rem(row, ROWS), s, -1e30)
        m = jnp.max(s, axis=-1, keepdims=True)
        w = jnp.exp2((s - m) * SCALE).astype(jnp.bfloat16)
        return m, jnp.dot(w, vaug[i], preferred_element_type=jnp.float32)

    def later(i, k, before):
        s = scores(i, k)
        m = jnp.maximum(before, jnp.max(s, axis=-1, keepdims=True))
        w = jnp.exp2((s - m) * SCALE).astype(jnp.bfloat16)
        return m, jnp.exp2((before - m) * SCALE), jnp.dot(w, vaug[k], preferred_element_type=jnp.float32)

    def keep(j, m, total):
        acc[j] = total
        top[j] = jnp.broadcast_to(m, (UNIT, HEAD_SIZE))

    @pl.loop(0, NZ // 2)
    def _(u):
        even, odd = 2 * u, 2 * u + 1
        m0, t0 = first(even)
        m1, t1 = first(odd)
        m1, fade, more = later(odd, even, m1)
        keep(0, m0, t0)
        keep(1, m1, t1 * fade + more)
        at = pl.multiple_of(even * CHUNK + block * ROWS, ROWS)
        head_doc = docs[:, pl.ds(at, ROWS)][:, :1]
        start = jnp.sum((docs[...] < head_doc).astype(jnp.int32))

        @pl.loop(start // CHUNK, even)
        def _(k):
            m0, f0, t0 = later(even, k, top[0][:, :1])
            m1, f1, t1 = later(odd, k, top[1][:, :1])
            keep(0, m0, acc[0] * f0 + t0)
            keep(1, m1, acc[1] * f1 + t1)

        for j in range(2):
            done = (acc[j][:, :HEAD_SIZE] / acc[j][:, HEAD_SIZE:]).astype(jnp.bfloat16)
            for g in range(2):
                out[2 * u + j, :, g * HEAD_SIZE : (g + 1) * HEAD_SIZE] = done[g * ROWS : (g + 1) * ROWS]


def give_back(o, scored, out, marks, send, recv, s_send, s_recv):
    x, z, y, c = place()
    xn, xp = lax.rem(x + 1, PHASES), lax.rem(x + PHASES - 1, PHASES)
    barrier = pltpu.get_barrier_semaphore()
    for d in range(NZ):
        pl.semaphore_signal(
            barrier, inc=1, device_id=device(xp, lax.rem(z + d, NZ), y, c), device_id_type=MESH
        )
    pl.semaphore_wait(barrier, NZ)
    started = []
    for d in reversed(ORDER):
        to = lax.rem(z + d, NZ)
        copy = remote(
            o.at[to], out.at[:, pl.ds(pl.multiple_of(z * WIDTH, WIDTH), WIDTH)],
            send.at[d], recv.at[z], device(xn, to, y, c),
        )
        copy.start()
        started.append(copy)
    copy = remote(scored, marks, s_send, s_recv, device(xn, z, y, c))
    copy.start()
    copy.wait()
    for d in range(NZ):
        at = lax.rem(z + d, NZ)
        ref = out.at[:, pl.ds(pl.multiple_of(at * WIDTH, WIDTH), WIDTH)]
        remote(ref, ref, send.at[d], recv.at[at], device(xn, z, y, c)).wait_recv()
    for copy in started:
        copy.wait_send()


def per_device(hidden, queries, key_value_weight, doc_ids, scored):
    first_row = lax.axis_index("ctx") * ROWS
    positions = first_row + jnp.arange(ROWS, dtype=jnp.int32)
    half = HEAD_SIZE // 2
    frequency = ROPE_BASE ** (-jnp.arange(half, dtype=jnp.float32) * 2.0 / HEAD_SIZE)
    angles = positions.astype(jnp.float32)[:, None] * frequency[None, :]
    dma = pltpu.SemaphoreType.DMA
    steps = MODEL_WIDTH // DEPTH_STEP
    kv, q8 = pl.pallas_call(
        gather,
        in_specs=[VMEM, ANY, ANY, VMEM, VMEM],
        out_specs=[ANY] * 2,
        out_shape=[
            jax.ShapeDtypeStruct((NC, NY, NZ, 2, ROWS, HEAD_SIZE), jnp.bfloat16),
            jax.ShapeDtypeStruct((NZ, ROWS, WIDTH), jnp.bfloat16),
        ],
        scratch_shapes=[
            pltpu.VMEM((MODEL_WIDTH, 1024), jnp.bfloat16),
            pltpu.VMEM((KEY_VALUE_HEADS, 2, ROWS, HEAD_SIZE), jnp.bfloat16),
            pltpu.VMEM((ROWS, 1024), jnp.float32),
            pltpu.VMEM((ROWS, WIDTH), jnp.bfloat16),
            dma((steps,)), dma((3,)),
            dma((NZ,)), dma((NZ,)), dma((NZ,)), dma((NZ,)),
            dma((2, NZ)), dma((2, NZ)), dma((2, NZ)), dma((2, NZ)), dma((NY, NZ)), dma((NY, NZ)),
        ],
        compiler_params=pltpu.CompilerParams(
            collective_id=0, has_side_effects=True, vmem_limit_bytes=40 << 20
        ),
        name="gather",
    )(hidden, key_value_weight, queries, jnp.cos(angles), jnp.sin(angles))

    o = pl.pallas_call(
        attend,
        in_specs=[VMEM] * 3,
        out_specs=VMEM,
        out_shape=jax.ShapeDtypeStruct((NZ, ROWS, WIDTH), jnp.bfloat16),
        scratch_shapes=[
            pltpu.VMEM((NZ, UNIT, 2 * HEAD_SIZE), jnp.bfloat16),
            pltpu.VMEM((NZ, 2 * HEAD_SIZE, CHUNK), jnp.bfloat16),
            pltpu.VMEM((NZ, CHUNK, 2 * HEAD_SIZE), jnp.bfloat16),
            pltpu.VMEM((2, UNIT, 2 * HEAD_SIZE), jnp.float32),
            pltpu.VMEM((2, UNIT, HEAD_SIZE), jnp.float32),
        ],
        compiler_params=pltpu.CompilerParams(vmem_limit_bytes=50 << 20),
        name="attend",
    )(kv, q8, doc_ids)

    back, marks = pl.pallas_call(
        give_back,
        in_specs=[ANY] * 2,
        out_specs=[ANY] * 2,
        out_shape=[
            jax.ShapeDtypeStruct((ROWS, NZ * WIDTH), jnp.bfloat16),
            jax.ShapeDtypeStruct(scored.shape, jnp.int32),
        ],
        scratch_shapes=[dma((NZ,)), dma((NZ,)), dma, dma],
        compiler_params=pltpu.CompilerParams(collective_id=1, has_side_effects=True),
        name="give_back",
    )(o, scored)
    return (back * marks[0].astype(jnp.bfloat16)[:, None])[None]


def solution(mesh):
    placed = (
        P("phase", "ctx", None),
        P("phase", "ctx", None),
        P("phase", None, None),
        P("phase", None),
        P("phase", "ctx"),
    )
    return jax.shard_map(
        per_device, mesh=mesh, in_specs=placed, out_specs=P("phase", "ctx", None), check_vma=False
    )
```

time: 298 us -> 102 us (0.34)
  waiting for transfers between devices: 113 us -> 0 us
  Pallas kernels: 0 us -> 93.8 us
  matrix products: 66.5 us -> 0 us
  local copies, waits for them, and re-layouts: 63.2 us -> 4.99 us
  other arithmetic: 39.1 us -> 2.88 us
  between operations: 13.6 us -> 0.07 us
    all_gather x1 -> x0, waiting for transfers between devices: 100 us -> none  [per_device(): collected_rows = lax.all_gather(stacked, 'ctx', axis=0, tiled=True)]
    pallas_call x0 -> x3, Pallas kernels: none -> 93.8 us  [the longest x1 45.4 us: per_device(): pl.pallas_call(gather, in_specs=[VMEM, ANY, ANY, VMEM, VMEM], out_specs=[...]
    dot_general x9 -> x0, matrix products: 66.5 us -> none  [the longest x4 32.2 us: per_device(): jnp.einsum('hgqk,khd->hgqd', weights, every_value_row[:, key_value_head:k...]
    slice x4 -> x0, local copies, waits for them, and re-layouts: 37.8 us -> none  [the longest x1 26.4 us: per_device(): key_part = every_key_row[:, key_value_head:key_value_head + 1]]
    reduce_sum x5 -> x0, other arithmetic: 33.4 us -> none  [the longest x4 31.9 us: per_device(): total = jnp.sum(expo, axis=-1)]
    reshape x4 -> x0, local copies, waits for them, and re-layouts: 24.3 us -> none  [the longest x1 12.5 us: per_device(): collected_rows[:, :key_value_width]]
    ppermute x1 -> x0, waiting for transfers between devices: 13.3 us -> none  [from_behind(): return lax.ppermute(block, axis, route)]
    and x1 -> x0, other arithmetic: 3.92 us -> none  [per_device(): (key_pos[None, :] <= token_positions[:, None]) & (sequence_docs[None, :]...]
  transfers between devices with their start and end apart: 2 -> 0, of which waited for: 2 -> 0; matrix products, arithmetic and copies ran while one was open for 1% -> 0% of each run, Pallas kernels for 0% -> 0%
where the time goes in v2:
time: 102 us
  Pallas kernels  93.8 us (92%)
  local copies, waits for them, and re-layouts  4.99 us (5%)
  other arithmetic  2.88 us (3%)
    pallas_call x1, Pallas kernels, per_device(): pl.pallas_call(gather, in_specs=[VMEM, ANY, ANY, VMEM, VMEM], out_specs=[...  45.4 us
    pallas_call x1, Pallas kernels, per_device(): pl.pallas_call(attend, in_specs=[VMEM] * 3, out_specs=VMEM, out_shape=jax...  27 us
    pallas_call x1, Pallas kernels, per_device(): pl.pallas_call(give_back, in_specs=[ANY] * 2, out_specs=[ANY] * 2, out_sh...  21.4 us
    unnamed x10, local copies, waits for them, and re-layouts  4.99 us

profile of v2, /device:TPU:1, one launch (start us, length us, event | category | flops | bytes accessed | tf_op | source)
XLA Modules:
  0.0 101.8 jit_solution(12464779278932981392)
XLA Ops:
  0.0 0.0 copy-start.4
  0.0 0.3 multiply_sine_fusion
  0.3 0.0 copy-start.2
  0.4 1.2 %copy-done.2 = bf16[1,128,4096]{2,1,0:T(8,128)(2,1)S(1)} copy-done((bf16[1,128,4096]{2,1,0:T(8,128)(2,1)S(1)}, bf16[1,128,4096]{2,1,0:T(8,128)(2,1)}, u32[]{:S(2)}) %copy-start.2) | copy-done | bytes 1048600
  1.6 0.0 copy-start.3
  1.6 1.0 %copy-done.3 = bf16[1,128,2048]{2,1,0:T(8,128)(2,1)S(1)} copy-done((bf16[1,128,2048]{2,1,0:T(8,128)(2,1)S(1)}, bf16[1,128,2048]{2,1,0:T(8,128)(2,1)}, u32[]{:S(2)}) %copy-start.3) | copy-done | bytes 524312
  2.6 45.4 %gather.1 = (bf16[2,4,8,2,128,128]{5,4,3,2,1,0:T(8,128)(2,1)S(1)}, bf16[8,128,256]{2,1,0:T(8,128)(2,1)S(1)}) custom-call(bf16[1,128,4096]{2,1,0:T(8,128)(2,1)S(1)} %copy-done.2, bf16[1,4096,1024]{2,1,0:T(8,128)(2,1)} %weight.1, bf16[1,128,2048]{2,1,0:T(8,128)(2,1)S(1)} %copy-done.3, f32[128,64]{1,0:T(8,128)S(1)} %get-tuple-element.14.cos_ref, ...), custom_call_target="tpu_custom_call" | custom-call | tf_op jit(solution)/shard_map/gather/pallas_call | solution.py:291
  48.1 0.0 copy-start
  48.1 1.9 %copy-done = bf16[2,4,8,2,128,128]{5,4,3,2,1,0:T(8,128)(2,1)} copy-done((bf16[2,4,8,2,128,128]{5,4,3,2,1,0:T(8,128)(2,1)}, bf16[2,4,8,2,128,128]{5,4,3,2,1,0:T(8,128)(2,1)S(1)}, u32[]{:S(2)}) %copy-start) | copy-done | bytes 4194328
  50.0 0.0 copy-done.4
  50.0 27.0 %attend.1.o = bf16[8,128,256]{2,1,0:T(8,128)(2,1)S(1)} custom-call(bf16[2,4,8,2,128,128]{5,4,3,2,1,0:T(8,128)(2,1)} %copy-done, bf16[8,128,256]{2,1,0:T(8,128)(2,1)S(1)} %get-tuple-element.10.q8, s32[1,8192]{1,0:T(1,128)S(1)} %copy-done.4), custom_call_target="tpu_custom_call" | custom-call | tf_op jit(solution)/shard_map/attend/pallas_call | solution.py:314
  77.0 0.0 copy-start.1
  77.0 0.8 copy-done.1
  77.8 21.4 %give_back.1 = (bf16[128,2048]{1,0:T(8,128)(2,1)}, s32[1,128]{1,0:T(1,128)}) custom-call(bf16[8,128,256]{2,1,0:T(8,128)(2,1)} %copy-done.1, s32[1,128]{1,0:T(1,128)} %scored.1), custom_call_target="tpu_custom_call" | custom-call | tf_op jit(solution)/shard_map/give_back/pallas_call | solution.py:330
  99.2 0.6 convert_bitcast_fusion
  99.8 1.9 %multiply_bitcast_fusion = bf16[1,128,2048]{2,1,0:T(8,128)(2,1)} fusion(bf16[128,2048]{1,0:T(8,128)(2,1)} %get-tuple-element.11, bf16[128]{0:T(256)(128)(2,1)S(1)} %convert_bitcast_fusion), kind=kLoop, calls=%fused_computation | loop fusion | flops 262144 | bytes 1048832 | tf_op jit(solution)/shard_map/broadcast_in_dim | solution.py:342
  (2 shorter events, 0.0 us)
Async XLA Ops:
  0.0 50.0 %copy-start.4 = (s32[1,8192]{1,0:T(1,128)S(1)}, s32[1,8192]{1,0:T(1,128)}, u32[]{:S(2)}) copy-start(s32[1,8192]{1,0:T(1,128)} %docs.1) | copy-start | bytes 98308
  0.3 1.2 %copy-start.2 = (bf16[1,128,4096]{2,1,0:T(8,128)(2,1)S(1)}, bf16[1,128,4096]{2,1,0:T(8,128)(2,1)}, u32[]{:S(2)}) copy-start(bf16[1,128,4096]{2,1,0:T(8,128)(2,1)} %hidden.1) | copy-start | bytes 3145732
  1.6 1.0 %copy-start.3 = (bf16[1,128,2048]{2,1,0:T(8,128)(2,1)S(1)}, bf16[1,128,2048]{2,1,0:T(8,128)(2,1)}, u32[]{:S(2)}) copy-start(bf16[1,128,2048]{2,1,0:T(8,128)(2,1)} %q.1) | copy-start | bytes 1572868
  48.1 1.9 %copy-start = (bf16[2,4,8,2,128,128]{5,4,3,2,1,0:T(8,128)(2,1)}, bf16[2,4,8,2,128,128]{5,4,3,2,1,0:T(8,128)(2,1)S(1)}, u32[]{:S(2)}) copy-start(bf16[2,4,8,2,128,128]{5,4,3,2,1,0:T(8,128)(2,1)S(1)} %get-tuple-element.9.kv) | copy-start | bytes 12582916
  77.0 0.8 copy-start.1

commit v3 on v2

--- a/solution.py
+++ b/solution.py
@@ -46,11 +46,13 @@
 
 def gather(
     hidden, weight, q, cos_ref, sin_ref, kv, q8,
-    wbuf, kvp, acc, own, w_sem, l_sem,
+    wbuf, hbuf, kvp, acc, own, w_sem, l_sem,
     a_send, a_recv, q_send, q_recv, up_send, up_recv, dn_send, dn_recv, p_send, p_recv,
 ):
     x, z, y, c = place()
     yu, yd = lax.rem(y + 1, NY), lax.rem(y + NY - 1, NY)
+    fetch = pltpu.make_async_copy(hidden.at[0], hbuf, l_sem.at[3])
+    fetch.start()
     loads = []
     for i in range(MODEL_WIDTH // DEPTH_STEP):
         part = pl.ds(i * DEPTH_STEP, DEPTH_STEP)
@@ -75,13 +77,17 @@
     def columns(at):
         return q.at[0, :, pl.ds(pl.multiple_of(at * WIDTH, WIDTH), WIDTH)]
 
-    for d in ORDER[1:]:
+    def ask(d):
         to = lax.rem(z + d, NZ)
         go(remote(columns(to), q8.at[z], q_send.at[d], q_recv.at[z], device(x, to, y, c)))
+
+    for d in (4, 3, 5):
+        ask(d)
     keep = pltpu.make_async_copy(columns(z), own, l_sem.at[0])
     keep.start()
 
-    wide = hidden[0].astype(jnp.float32)
+    fetch.wait()
+    wide = hbuf[...].astype(jnp.float32)
     scale = lax.rsqrt(jnp.mean(wide * wide, axis=-1, keepdims=True) + 1e-05)
     rows = (wide * scale).astype(jnp.bfloat16)
     for i, load in enumerate(loads):
@@ -112,6 +118,8 @@
     for d in ORDER[1:]:
         to = lax.rem(z + d, NZ)
         go(remote(kvp.at[to // 2], kv.at[c, y, z], a_send.at[d], a_recv.at[z], device(x, to, y, c)))
+    for d in (2, 6, 1, 7):
+        ask(d)
     mine = kvp.at[z // 2]
     home = pltpu.make_async_copy(mine, kv.at[c, y, z], l_sem.at[2])
     home.start()
@@ -178,8 +186,26 @@
 UNIT = 2 * ROWS
 
 
-def attend(kv, q8, docs, out, qaug, kaug, vaug, acc, top):
+def attend(
+    kv, q8, docs, scored, out, marks,
+    qaug, kaug, vaug, acc, top, o, l_sem, send, recv, s_send, s_recv,
+):
     x, z, y, c = place()
+    xn, xp = lax.rem(x + 1, PHASES), lax.rem(x + PHASES - 1, PHASES)
+    loads = []
+    for p in range(NY):
+        for c2 in range(NC):
+            b = p * NC + c2
+            keys = pl.ds(b * ROWS, ROWS)
+            for part, dst in ((0, kaug.at[:, :HEAD_SIZE, keys]), (1, vaug.at[:, keys, :HEAD_SIZE])):
+                load = pltpu.make_async_copy(kv.at[c2, p, :, part], dst, l_sem.at[2 * b + part])
+                load.start()
+                loads.append(load)
+    barrier = pltpu.get_barrier_semaphore()
+    for d in range(NZ):
+        pl.semaphore_signal(
+            barrier, inc=1, device_id=device(xp, lax.rem(z + d, NZ), y, c), device_id_type=MESH
+        )
     lanes = lax.broadcasted_iota(jnp.int32, (ROWS, ROWS), 1)
     sublanes = lax.broadcasted_iota(jnp.int32, (ROWS, ROWS), 0)
     apart = jnp.where(lanes == sublanes, 0.0, FAR).astype(jnp.bfloat16)
@@ -196,13 +222,17 @@
             qaug[i, g * ROWS : (g + 1) * ROWS, :HEAD_SIZE] = q8[i, :, g * HEAD_SIZE : (g + 1) * HEAD_SIZE]
             qaug[i, g * ROWS : (g + 1) * ROWS, HEAD_SIZE:] = away
         vaug[i, :, HEAD_SIZE:] = jnp.ones((CHUNK, HEAD_SIZE), jnp.bfloat16)
-        for p in range(NY):
-            for c2 in range(NC):
-                b = (p * NC + c2) * ROWS
-                at = pl.multiple_of(i * CHUNK + b, ROWS)
-                kaug[i, :HEAD_SIZE, b : b + ROWS] = kv[c2, p, i, 0]
-                kaug[i, HEAD_SIZE:, b : b + ROWS] = (sublanes == docs[:, pl.ds(at, ROWS)]).astype(jnp.bfloat16)
-                vaug[i, b : b + ROWS, :HEAD_SIZE] = kv[c2, p, i, 1]
+        for b in range(NY * NC):
+            at = pl.multiple_of(i * CHUNK + b * ROWS, ROWS)
+            kaug[i, HEAD_SIZE:, b * ROWS : (b + 1) * ROWS] = (
+                sublanes == docs[:, pl.ds(at, ROWS)]
+            ).astype(jnp.bfloat16)
+
+    for load in loads:
+        load.wait()
+    pl.semaphore_wait(barrier, NZ)
+    mark = remote(scored, marks, s_send, s_recv, device(xn, z, y, c))
+    mark.start()
 
     def scores(i, k):
         return jnp.dot(qaug[i], kaug[k], preferred_element_type=jnp.float32)
@@ -226,19 +256,19 @@
         acc[j] = total
         top[j] = jnp.broadcast_to(m, (UNIT, HEAD_SIZE))
 
+    mine = out.at[:, pl.ds(pl.multiple_of(z * WIDTH, WIDTH), WIDTH)]
+
     @pl.loop(0, NZ // 2)
-    def _(u):
+    def _(n):
+        u = lax.rem(z // 2 + n, NZ // 2)
         even, odd = 2 * u, 2 * u + 1
         m0, t0 = first(even)
         m1, t1 = first(odd)
         m1, fade, more = later(odd, even, m1)
         keep(0, m0, t0)
         keep(1, m1, t1 * fade + more)
-        at = pl.multiple_of(even * CHUNK + block * ROWS, ROWS)
-        head_doc = docs[:, pl.ds(at, ROWS)][:, :1]
-        start = jnp.sum((docs[...] < head_doc).astype(jnp.int32))
-
-        @pl.loop(start // CHUNK, even)
+
+        @pl.loop(0, even)
         def _(k):
             m0, f0, t0 = later(even, k, top[0][:, :1])
             m1, f1, t1 = later(odd, k, top[1][:, :1])
@@ -248,36 +278,19 @@
         for j in range(2):
             done = (acc[j][:, :HEAD_SIZE] / acc[j][:, HEAD_SIZE:]).astype(jnp.bfloat16)
             for g in range(2):
-                out[2 * u + j, :, g * HEAD_SIZE : (g + 1) * HEAD_SIZE] = done[g * ROWS : (g + 1) * ROWS]
-
-
-def give_back(o, scored, out, marks, send, recv, s_send, s_recv):
-    x, z, y, c = place()
-    xn, xp = lax.rem(x + 1, PHASES), lax.rem(x + PHASES - 1, PHASES)
-    barrier = pltpu.get_barrier_semaphore()
-    for d in range(NZ):
-        pl.semaphore_signal(
-            barrier, inc=1, device_id=device(xp, lax.rem(z + d, NZ), y, c), device_id_type=MESH
-        )
-    pl.semaphore_wait(barrier, NZ)
-    started = []
-    for d in reversed(ORDER):
-        to = lax.rem(z + d, NZ)
-        copy = remote(
-            o.at[to], out.at[:, pl.ds(pl.multiple_of(z * WIDTH, WIDTH), WIDTH)],
-            send.at[d], recv.at[z], device(xn, to, y, c),
-        )
-        copy.start()
-        started.append(copy)
-    copy = remote(scored, marks, s_send, s_recv, device(xn, z, y, c))
-    copy.start()
-    copy.wait()
+                o[2 * n + j, :, g * HEAD_SIZE : (g + 1) * HEAD_SIZE] = done[g * ROWS : (g + 1) * ROWS]
+        for j in range(2):
+            remote(
+                o.at[2 * n + j], mine, send.at[2 * n + j], recv.at[z], device(xn, 2 * u + j, y, c)
+            ).start()
+
     for d in range(NZ):
         at = lax.rem(z + d, NZ)
         ref = out.at[:, pl.ds(pl.multiple_of(at * WIDTH, WIDTH), WIDTH)]
         remote(ref, ref, send.at[d], recv.at[at], device(xn, z, y, c)).wait_recv()
-    for copy in started:
-        copy.wait_send()
+    for n in range(NZ):
+        remote(o.at[n], mine, send.at[n], recv.at[z], device(xn, z, y, c)).wait_send()
+    mark.wait()
 
 
 def per_device(hidden, queries, key_value_weight, doc_ids, scored):
@@ -290,7 +303,7 @@
     steps = MODEL_WIDTH // DEPTH_STEP
     kv, q8 = pl.pallas_call(
         gather,
-        in_specs=[VMEM, ANY, ANY, VMEM, VMEM],
+        in_specs=[ANY, ANY, ANY, VMEM, VMEM],
         out_specs=[ANY] * 2,
         out_shape=[
             jax.ShapeDtypeStruct((NC, NY, NZ, 2, ROWS, HEAD_SIZE), jnp.bfloat16),
@@ -298,10 +311,11 @@
         ],
         scratch_shapes=[
             pltpu.VMEM((MODEL_WIDTH, 1024), jnp.bfloat16),
+            pltpu.VMEM((ROWS, MODEL_WIDTH), jnp.bfloat16),
             pltpu.VMEM((KEY_VALUE_HEADS, 2, ROWS, HEAD_SIZE), jnp.bfloat16),
             pltpu.VMEM((ROWS, 1024), jnp.float32),
             pltpu.VMEM((ROWS, WIDTH), jnp.bfloat16),
-            dma((steps,)), dma((3,)),
+            dma((steps,)), dma((4,)),
             dma((NZ,)), dma((NZ,)), dma((NZ,)), dma((NZ,)),
             dma((2, NZ)), dma((2, NZ)), dma((2, NZ)), dma((2, NZ)), dma((NY, NZ)), dma((NY, NZ)),
         ],
@@ -311,34 +325,28 @@
         name="gather",
     )(hidden, key_value_weight, queries, jnp.cos(angles), jnp.sin(angles))
 
-    o = pl.pallas_call(
+    back, marks = pl.pallas_call(
         attend,
-        in_specs=[VMEM] * 3,
-        out_specs=VMEM,
-        out_shape=jax.ShapeDtypeStruct((NZ, ROWS, WIDTH), jnp.bfloat16),
+        in_specs=[ANY, VMEM, VMEM, ANY],
+        out_specs=[ANY] * 2,
+        out_shape=[
+            jax.ShapeDtypeStruct((ROWS, NZ * WIDTH), jnp.bfloat16),
+            jax.ShapeDtypeStruct(scored.shape, jnp.int32),
+        ],
         scratch_shapes=[
             pltpu.VMEM((NZ, UNIT, 2 * HEAD_SIZE), jnp.bfloat16),
             pltpu.VMEM((NZ, 2 * HEAD_SIZE, CHUNK), jnp.bfloat16),
             pltpu.VMEM((NZ, CHUNK, 2 * HEAD_SIZE), jnp.bfloat16),
             pltpu.VMEM((2, UNIT, 2 * HEAD_SIZE), jnp.float32),
             pltpu.VMEM((2, UNIT, HEAD_SIZE), jnp.float32),
+            pltpu.VMEM((NZ, ROWS, WIDTH), jnp.bfloat16),
+            dma((2 * NY * NC,)), dma((NZ,)), dma((NZ,)), dma, dma,
         ],
-        compiler_params=pltpu.CompilerParams(vmem_limit_bytes=50 << 20),
+        compiler_params=pltpu.CompilerParams(
+            collective_id=1, has_side_effects=True, vmem_limit_bytes=50 << 20
+        ),
         name="attend",
-    )(kv, q8, doc_ids)
-
-    back, marks = pl.pallas_call(
-        give_back,
-        in_specs=[ANY] * 2,
-        out_specs=[ANY] * 2,
-        out_shape=[
-            jax.ShapeDtypeStruct((ROWS, NZ * WIDTH), jnp.bfloat16),
-            jax.ShapeDtypeStruct(scored.shape, jnp.int32),
-        ],
-        scratch_shapes=[dma((NZ,)), dma((NZ,)), dma, dma],
-        compiler_params=pltpu.CompilerParams(collective_id=1, has_side_effects=True),
-        name="give_back",
-    )(o, scored)
+    )(kv, q8, doc_ids, scored)
     return (back * marks[0].astype(jnp.bfloat16)[:, None])[None]
 
 

time: 102 us -> 86.3 us (0.85)
  Pallas kernels: 93.8 us -> 80.7 us
  other arithmetic: 2.88 us -> 1.23 us
    pallas_call x3 -> x2, Pallas kernels: 93.8 us -> 80.7 us  [the longest x1 41.6 us: per_device(): pl.pallas_call(gather, in_specs=[ANY, ANY, ANY, VMEM, VMEM], out_specs=[A...]
    broadcast_in_dim x1, other arithmetic: 1.94 us -> 0.9 us  [per_device(): return (back * marks[0].astype(jnp.bfloat16)[:, None])[None]]
where the time goes in v3:
time: 86.3 us; the launch traced here: 86.2 us
  Pallas kernels  80.7 us (94%)
  local copies, waits for them, and re-layouts  4.2 us (5%)
  other arithmetic  1.23 us (1%)
    pallas_call x1, Pallas kernels, per_device(): pl.pallas_call(gather, in_specs=[ANY, ANY, ANY, VMEM, VMEM], out_specs=[A...  41.6 us
    pallas_call x1, Pallas kernels, per_device(): pl.pallas_call(attend, in_specs=[ANY, VMEM, VMEM, ANY], out_specs=[ANY] *...  39.1 us
    unnamed x10, local copies, waits for them, and re-layouts  4.2 us

profile of v3, /device:TPU:1, one launch (start us, length us, event | category | flops | bytes accessed | tf_op | source)
XLA Modules:
  0.0 86.2 jit_solution(11590319162535930252)
XLA Ops:
  0.0 0.0 copy-start.4
  0.0 0.0 copy-start.3
  0.0 0.3 multiply_sine_fusion
  0.3 0.0 copy-start.1
  0.4 1.2 %copy-done.1 = bf16[1,128,4096]{2,1,0:T(8,128)(2,1)S(1)} copy-done((bf16[1,128,4096]{2,1,0:T(8,128)(2,1)S(1)}, bf16[1,128,4096]{2,1,0:T(8,128)(2,1)}, u32[]{:S(2)}) %copy-start.1) | copy-done | bytes 1048600
  1.6 0.0 copy-start.2
  1.6 1.0 %copy-done.2 = bf16[1,128,2048]{2,1,0:T(8,128)(2,1)S(1)} copy-done((bf16[1,128,2048]{2,1,0:T(8,128)(2,1)S(1)}, bf16[1,128,2048]{2,1,0:T(8,128)(2,1)}, u32[]{:S(2)}) %copy-start.2) | copy-done | bytes 524312
  2.6 41.6 %gather.1 = (bf16[2,4,8,2,128,128]{5,4,3,2,1,0:T(8,128)(2,1)S(1)}, bf16[8,128,256]{2,1,0:T(8,128)(2,1)S(1)}) custom-call(bf16[1,128,4096]{2,1,0:T(8,128)(2,1)S(1)} %copy-done.1, bf16[1,4096,1024]{2,1,0:T(8,128)(2,1)} %weight.1, bf16[1,128,2048]{2,1,0:T(8,128)(2,1)S(1)} %copy-done.2, f32[128,64]{1,0:T(8,128)S(1)} %get-tuple-element.14.cos_ref, ...), custom_call_target="tpu_custom_call" | custom-call | tf_op jit(solution)/shard_map/gather/pallas_call | solution.py:304
  44.2 0.0 copy-start
  44.2 1.9 %copy-done = bf16[2,4,8,2,128,128]{5,4,3,2,1,0:T(8,128)(2,1)} copy-done((bf16[2,4,8,2,128,128]{5,4,3,2,1,0:T(8,128)(2,1)}, bf16[2,4,8,2,128,128]{5,4,3,2,1,0:T(8,128)(2,1)S(1)}, u32[]{:S(2)}) %copy-start) | copy-done | bytes 4194328
  46.1 0.0 copy-done.4
  46.1 0.0 copy-done.3
  46.1 39.1 %attend.1 = (bf16[128,2048]{1,0:T(8,128)(2,1)S(1)}, s32[1,128]{1,0:T(1,128)S(1)}) custom-call(bf16[2,4,8,2,128,128]{5,4,3,2,1,0:T(8,128)(2,1)} %copy-done, bf16[8,128,256]{2,1,0:T(8,128)(2,1)S(1)} %get-tuple-element.10.q8, s32[1,8192]{1,0:T(1,128)S(1)} %copy-done.3, s32[1,128]{1,0:T(1,128)S(1)} %copy-done.4), custom_call_target="tpu_custom_call" | custom-call | tf_op jit(solution)/shard_map/attend/pallas_call | solution.py:328
  85.3 0.9 %multiply_bitcast_fusion = bf16[1,128,2048]{2,1,0:T(8,128)(2,1)} fusion(bf16[128,2048]{1,0:T(8,128)(2,1)S(1)} %get-tuple-element.11, bf16[128]{0:T(256)(128)(2,1)S(1)} %convert_bitcast_fusion), kind=kLoop, calls=%fused_computation | loop fusion | flops 262144 | bytes 1048832 | tf_op jit(solution)/shard_map/broadcast_in_dim | solution.py:350
  (3 shorter events, 0.0 us)
Async XLA Ops:
  0.0 46.1 %copy-start.4 = (s32[1,128]{1,0:T(1,128)S(1)}, s32[1,128]{1,0:T(1,128)}, u32[]{:S(2)}) copy-start(s32[1,128]{1,0:T(1,128)} %scored.1) | copy-start | bytes 1540
  0.0 46.1 %copy-start.3 = (s32[1,8192]{1,0:T(1,128)S(1)}, s32[1,8192]{1,0:T(1,128)}, u32[]{:S(2)}) copy-start(s32[1,8192]{1,0:T(1,128)} %docs.1) | copy-start | bytes 98308
  0.3 1.2 %copy-start.1 = (bf16[1,128,4096]{2,1,0:T(8,128)(2,1)S(1)}, bf16[1,128,4096]{2,1,0:T(8,128)(2,1)}, u32[]{:S(2)}) copy-start(bf16[1,128,4096]{2,1,0:T(8,128)(2,1)} %hidden.1) | copy-start | bytes 3145732
  1.6 1.0 %copy-start.2 = (bf16[1,128,2048]{2,1,0:T(8,128)(2,1)S(1)}, bf16[1,128,2048]{2,1,0:T(8,128)(2,1)}, u32[]{:S(2)}) copy-start(bf16[1,128,2048]{2,1,0:T(8,128)(2,1)} %q.1) | copy-start | bytes 1572868
  44.2 1.9 %copy-start = (bf16[2,4,8,2,128,128]{5,4,3,2,1,0:T(8,128)(2,1)}, bf16[2,4,8,2,128,128]{5,4,3,2,1,0:T(8,128)(2,1)S(1)}, u32[]{:S(2)}) copy-start(bf16[2,4,8,2,128,128]{5,4,3,2,1,0:T(8,128)(2,1)S(1)} %get-tuple-element.9.kv) | copy-start | bytes 12582916

commit v4 on v3

--- a/solution.py
+++ b/solution.py
@@ -320,7 +320,7 @@
             dma((2, NZ)), dma((2, NZ)), dma((2, NZ)), dma((2, NZ)), dma((NY, NZ)), dma((NY, NZ)),
         ],
         compiler_params=pltpu.CompilerParams(
-            collective_id=0, has_side_effects=True, vmem_limit_bytes=40 << 20
+            collective_id=0, has_side_effects=True, vmem_limit_bytes=66781184
         ),
         name="gather",
     )(hidden, key_value_weight, queries, jnp.cos(angles), jnp.sin(angles))
@@ -343,7 +343,7 @@
             dma((2 * NY * NC,)), dma((NZ,)), dma((NZ,)), dma, dma,
         ],
         compiler_params=pltpu.CompilerParams(
-            collective_id=1, has_side_effects=True, vmem_limit_bytes=50 << 20
+            collective_id=1, has_side_effects=True, vmem_limit_bytes=66781184
         ),
         name="attend",
     )(kv, q8, doc_ids, scored)

time: 86.3 us -> 87.4 us (1.013)
  local copies, waits for them, and re-layouts: 4.2 us -> 0 us
  Pallas kernels: 80.7 us -> 83.7 us
  other arithmetic: 1.23 us -> 3.51 us
    unnamed x10 -> x0, local copies, waits for them, and re-layouts: 4.2 us -> none
    pallas_call x1, Pallas kernels: 41.6 us -> 43.6 us  [per_device(): pl.pallas_call(gather, in_specs=[ANY, ANY, ANY, VMEM, VMEM], out_specs=[A...]
    broadcast_in_dim x1, other arithmetic: 0.9 us -> 1.94 us  [per_device(): return (back * marks[0].astype(jnp.bfloat16)[:, None])[None]]
    pallas_call x1, Pallas kernels: 39.1 us -> 40.1 us  [per_device(): pl.pallas_call(attend, in_specs=[ANY, VMEM, VMEM, ANY], out_specs=[ANY] *...]
where the time goes in v4:
time: 87.4 us; the launch traced here: 87.2 us
  Pallas kernels  83.7 us (96%)
  other arithmetic  3.51 us (4%)
    pallas_call x1, Pallas kernels, per_device(): pl.pallas_call(gather, in_specs=[ANY, ANY, ANY, VMEM, VMEM], out_specs=[A...  43.6 us
    pallas_call x1, Pallas kernels, per_device(): pl.pallas_call(attend, in_specs=[ANY, VMEM, VMEM, ANY], out_specs=[ANY] *...  40.1 us
    broadcast_in_dim x1, other arithmetic, per_device(): return (back * marks[0].astype(jnp.bfloat16)[:, None])[None]  1.94 us

profile of v4, /device:TPU:1, one launch (start us, length us, event | category | flops | bytes accessed | tf_op | source)
XLA Modules:
  0.0 87.2 jit_solution(5559705920906634845)
XLA Ops:
  0.0 1.0 %multiply_sine_fusion = (f32[128,64]{1,0:T(8,128)}, f32[128,64]{1,0:T(8,128)}) fusion(f32[64]{0:T(128)S(1)} %multiply_power_fusion, f32[128]{0:T(128)S(1)} %add_convert_fusion), kind=kLoop, calls=%fused_computation.1 | loop fusion | flops 8192 | bytes 66304 | tf_op jit(solution)/shard_map/sin | solution.py:326
  1.0 43.6 %gather.1 = (bf16[2,4,8,2,128,128]{5,4,3,2,1,0:T(8,128)(2,1)}, bf16[8,128,256]{2,1,0:T(8,128)(2,1)}) custom-call(bf16[1,128,4096]{2,1,0:T(8,128)(2,1)} %hidden.1, bf16[1,4096,1024]{2,1,0:T(8,128)(2,1)} %weight.1, bf16[1,128,2048]{2,1,0:T(8,128)(2,1)} %q.1, f32[128,64]{1,0:T(8,128)} %get-tuple-element.14.cos_ref, f32[128,64]{1,0:T(8,128)} %get-tuple-element.13.sin_ref), custom_call_target="tpu_custom_call" | custom-call | tf_op jit(solution)/shard_map/gather/pallas_call | solution.py:304
  44.6 40.1 %attend.1 = (bf16[128,2048]{1,0:T(8,128)(2,1)}, s32[1,128]{1,0:T(1,128)}) custom-call(bf16[2,4,8,2,128,128]{5,4,3,2,1,0:T(8,128)(2,1)} %get-tuple-element.9.kv, bf16[8,128,256]{2,1,0:T(8,128)(2,1)} %get-tuple-element.10.q8, s32[1,8192]{1,0:T(1,128)} %docs.1, s32[1,128]{1,0:T(1,128)} %scored.1), custom_call_target="tpu_custom_call" | custom-call | tf_op jit(solution)/shard_map/attend/pallas_call | solution.py:328
  84.7 0.6 convert_bitcast_fusion
  85.3 1.9 %multiply_bitcast_fusion = bf16[1,128,2048]{2,1,0:T(8,128)(2,1)} fusion(bf16[128,2048]{1,0:T(8,128)(2,1)} %get-tuple-element.11, bf16[128]{0:T(256)(128)(2,1)S(1)} %convert_bitcast_fusion), kind=kLoop, calls=%fused_computation | loop fusion | flops 262144 | bytes 1048832 | tf_op jit(solution)/shard_map/broadcast_in_dim | solution.py:350
  (2 shorter events, 0.0 us)

commit v5 on v3

--- a/solution.py
+++ b/solution.py
@@ -343,7 +343,7 @@
             dma((2 * NY * NC,)), dma((NZ,)), dma((NZ,)), dma, dma,
         ],
         compiler_params=pltpu.CompilerParams(
-            collective_id=1, has_side_effects=True, vmem_limit_bytes=50 << 20
+            collective_id=1, has_side_effects=True, vmem_limit_bytes=32 << 20
         ),
         name="attend",
     )(kv, q8, doc_ids, scored)

time: 86.3 us -> 85.4 us (0.990)
  local copies, waits for them, and re-layouts: 4.2 us -> 2.27 us
  Pallas kernels: 80.7 us -> 81.7 us
    unnamed x10 -> x8, local copies, waits for them, and re-layouts: 4.2 us -> 2.27 us
    pallas_call x1, Pallas kernels: 39.1 us -> 40.1 us  [per_device(): pl.pallas_call(attend, in_specs=[ANY, VMEM, VMEM, ANY], out_specs=[ANY] *...]
where the time goes in v5:
time: 85.4 us; the launch traced here: 85.2 us
  Pallas kernels  81.7 us (96%)
  local copies, waits for them, and re-layouts  2.27 us (3%)
  other arithmetic  1.23 us (1%)
    pallas_call x1, Pallas kernels, per_device(): pl.pallas_call(gather, in_specs=[ANY, ANY, ANY, VMEM, VMEM], out_specs=[A...  41.6 us
    pallas_call x1, Pallas kernels, per_device(): pl.pallas_call(attend, in_specs=[ANY, VMEM, VMEM, ANY], out_specs=[ANY] *...  40.1 us
    unnamed x8, local copies, waits for them, and re-layouts  2.27 us

profile of v5, /device:TPU:1, one launch (start us, length us, event | category | flops | bytes accessed | tf_op | source)
XLA Modules:
  0.0 85.2 jit_solution(2418271156584918966)
XLA Ops:
  0.0 0.0 copy-start.3
  0.0 0.0 copy-start.2
  0.0 0.3 multiply_sine_fusion
  0.3 0.0 copy-start
  0.4 1.2 %copy-done = bf16[1,128,4096]{2,1,0:T(8,128)(2,1)S(1)} copy-done((bf16[1,128,4096]{2,1,0:T(8,128)(2,1)S(1)}, bf16[1,128,4096]{2,1,0:T(8,128)(2,1)}, u32[]{:S(2)}) %copy-start) | copy-done | bytes 1048600
  1.6 0.0 copy-start.1
  1.6 1.0 %copy-done.1 = bf16[1,128,2048]{2,1,0:T(8,128)(2,1)S(1)} copy-done((bf16[1,128,2048]{2,1,0:T(8,128)(2,1)S(1)}, bf16[1,128,2048]{2,1,0:T(8,128)(2,1)}, u32[]{:S(2)}) %copy-start.1) | copy-done | bytes 524312
  2.6 41.6 %gather.1 = (bf16[2,4,8,2,128,128]{5,4,3,2,1,0:T(8,128)(2,1)S(1)}, bf16[8,128,256]{2,1,0:T(8,128)(2,1)S(1)}) custom-call(bf16[1,128,4096]{2,1,0:T(8,128)(2,1)S(1)} %copy-done, bf16[1,4096,1024]{2,1,0:T(8,128)(2,1)} %weight.1, bf16[1,128,2048]{2,1,0:T(8,128)(2,1)S(1)} %copy-done.1, f32[128,64]{1,0:T(8,128)S(1)} %get-tuple-element.14.cos_ref, ...), custom_call_target="tpu_custom_call" | custom-call | tf_op jit(solution)/shard_map/gather/pallas_call | solution.py:304
  44.2 0.0 copy-done.3
  44.2 0.0 copy-done.2
  44.2 40.1 %attend.1 = (bf16[128,2048]{1,0:T(8,128)(2,1)S(1)}, s32[1,128]{1,0:T(1,128)S(1)}) custom-call(bf16[2,4,8,2,128,128]{5,4,3,2,1,0:T(8,128)(2,1)S(1)} %get-tuple-element.9.kv, bf16[8,128,256]{2,1,0:T(8,128)(2,1)S(1)} %get-tuple-element.10.q8, s32[1,8192]{1,0:T(1,128)S(1)} %copy-done.2, s32[1,128]{1,0:T(1,128)S(1)} %copy-done.3), custom_call_target="tpu_custom_call" | custom-call | tf_op jit(solution)/shard_map/attend/pallas_call | solution.py:328
  84.3 0.9 %multiply_bitcast_fusion = bf16[1,128,2048]{2,1,0:T(8,128)(2,1)} fusion(bf16[128,2048]{1,0:T(8,128)(2,1)S(1)} %get-tuple-element.11, bf16[128]{0:T(256)(128)(2,1)S(1)} %convert_bitcast_fusion), kind=kLoop, calls=%fused_computation | loop fusion | flops 262144 | bytes 1048832 | tf_op jit(solution)/shard_map/broadcast_in_dim | solution.py:350
  (3 shorter events, 0.0 us)
Async XLA Ops:
  0.0 44.2 %copy-start.3 = (s32[1,128]{1,0:T(1,128)S(1)}, s32[1,128]{1,0:T(1,128)}, u32[]{:S(2)}) copy-start(s32[1,128]{1,0:T(1,128)} %scored.1) | copy-start | bytes 1540
  0.0 44.2 %copy-start.2 = (s32[1,8192]{1,0:T(1,128)S(1)}, s32[1,8192]{1,0:T(1,128)}, u32[]{:S(2)}) copy-start(s32[1,8192]{1,0:T(1,128)} %docs.1) | copy-start | bytes 98308
  0.3 1.2 %copy-start = (bf16[1,128,4096]{2,1,0:T(8,128)(2,1)S(1)}, bf16[1,128,4096]{2,1,0:T(8,128)(2,1)}, u32[]{:S(2)}) copy-start(bf16[1,128,4096]{2,1,0:T(8,128)(2,1)} %hidden.1) | copy-start | bytes 3145732
  1.6 1.0 %copy-start.1 = (bf16[1,128,2048]{2,1,0:T(8,128)(2,1)S(1)}, bf16[1,128,2048]{2,1,0:T(8,128)(2,1)}, u32[]{:S(2)}) copy-start(bf16[1,128,2048]{2,1,0:T(8,128)(2,1)} %q.1) | copy-start | bytes 1572868
